TPU v7x, 256 devices: a whole 4x4x8 slice. The times are simulated.
256 devices in a mesh: dom: 32 (over z_lo, y, core), st: 8 (over z_hi, x).
Axes of the slice: x: 4, y: 4, z: 8 (z_hi: 2, z_lo: 4; z = z_hi * 4 + z_lo), core: 2. Of those that a mesh axis runs over, the one named last changes fastest.
Arguments:
- start_states: bfloat16 [512, 114688], P('st', 'dom'), may hold values from -6 to 6
- stiffness: bfloat16 [512, 512], replicated, may hold values from -1 to 3
- cell_scale: float32 [256], P('dom'), may hold values from 0.5 to 2
- potential: float32 [114688], P('dom'), may hold values from -2 to 2
- connectivity: int32 [256, 512], P('dom'), may hold values from 0 to 3479, as said below
- shared_nodes: int32 [32, 2, 435], P('dom'), may hold values from 0 to 3479, as said below
- filter_bounds: float32 [2], replicated, may hold values from 3 to 60, as said below
Outputs:
- new_states: bfloat16 [512, 114688], P('st', 'dom')
Inputs may be any that keep to these rules, and one draw needn't show every extreme that they name: `connectivity`: for each domain, its cells' entries name every one of its 3480 local nodes; nodes of a domain are numbered in a drawn order; cells of a domain share nodes as hexahedral elements of order 7 do. shared_nodes[d, 1] and shared_nodes[d + 1, 0] list the same mesh nodes in the same order; within one domain the two lists are distinct nodes and disjoint. filter_bounds[0] < filter_bounds[1].
All inputs are finite; a program needn't handle non-finite values.
Results may differ from a plain program's by a relative error of at most 0.0049.
The roundings to bfloat16 on the way count: a program that leaves them out, or rounds other values in their place, can miss the bound.
Values may be sent and summed in bfloat16 or wider, within the bound.
A program may use at most 64 MiB of HBM per device.

v0:
```python
import functools
import jax
import jax.numpy as jnp
from jax import lax
from jax.experimental import pallas as pl
from jax.experimental.pallas import tpu as pltpu
from jax.sharding import PartitionSpec as P

f32 = jnp.float32
bf16 = jnp.bfloat16
DEGREE = 3
NS_ITERS = 3
CELLS = 8
NPC = 512
ENT = CELLS * NPC
LN = 3480
LNP = 3584
SH = 435
FACE = 512
SPEC = 1536
MESH_ID = pl.DeviceIdType.MESH


def one_hot_rows(row, count):
    ids = lax.broadcasted_iota(jnp.int32, (count, row.shape[1]), 0)
    return jnp.where(ids == row, 1.0, 0.0).astype(bf16)


def as_column(row):
    return jnp.transpose(jnp.broadcast_to(row, (128, 128)))


def contract_last(a, b):
    return lax.dot_general(a, b, (((1,), (1,)), ((), ())), preferred_element_type=f32)


def dot(a, b):
    return jnp.dot(a, b, preferred_element_type=f32)


def node_tables(conn, faces, oa, ob):
    total = jnp.zeros((128, 32), f32)
    seen = []
    for c in range(CELLS):
        seen.append(total)
        part = slice(c * NPC, (c + 1) * NPC)
        total = total + contract_last(oa[:, part], ob[:, part])
    place = lax.broadcasted_iota(jnp.int32, (1, FACE), 1)
    face_tabs = []
    for side in range(2):
        row = faces[side : side + 1]
        fa = one_hot_rows(lax.shift_right_arithmetic(row, 5), 128)
        fb = one_hot_rows(lax.bitwise_and(row, 31), 32)
        high = (fa * lax.shift_right_logical(place, 7).astype(f32).astype(bf16)).astype(bf16)
        low = (fa * lax.bitwise_and(place, 127).astype(f32).astype(bf16)).astype(bf16)
        face_tabs.append((contract_last(fa, fb), contract_last(high, fb), contract_last(low, fb)))
    (is_l, l_hi, l_lo), (is_r, r_hi, r_lo) = face_tabs
    other = jnp.where((total > 1.5) & (is_l + is_r < 0.5), 1.0, 0.0)
    before_b = jnp.where(
        lax.broadcasted_iota(jnp.int32, (32, 32), 0) < lax.broadcasted_iota(jnp.int32, (32, 32), 1), 1.0, 0.0
    ).astype(bf16)
    before_a = jnp.where(
        lax.broadcasted_iota(jnp.int32, (128, 128), 1) < lax.broadcasted_iota(jnp.int32, (128, 128), 0), 1.0, 0.0
    ).astype(bf16)
    row_sum = jnp.broadcast_to(jnp.sum(other, axis=1, keepdims=True), (128, 32))
    rank = dot(other.astype(bf16), before_b) + dot(before_a, row_sum.astype(bf16))
    rank = rank.astype(jnp.int32)
    slot = rank + jnp.where(rank < FACE - SH, SH, 2 * SH)
    o_hi = lax.shift_right_logical(slot, 7).astype(f32)
    o_lo = lax.bitwise_and(slot, 127).astype(f32)
    hi = jnp.where(is_l > 0.5, l_hi, jnp.where(is_r > 0.5, r_hi + FACE // 128, jnp.where(other > 0.5, o_hi, -1.0)))
    lo = jnp.where(is_l > 0.5, l_lo, jnp.where(is_r > 0.5, r_lo, jnp.where(other > 0.5, o_lo, 0.0)))
    return hi, lo, total, seen


def at_entries(tables, oa, ob):
    stacked = jnp.concatenate(tables, axis=1).astype(bf16)
    picked = lax.dot_general(stacked, oa, (((0,), (0,)), ((), ())), preferred_element_type=f32)
    wide = ob.astype(f32)
    return [
        jnp.sum(picked[32 * k : 32 * (k + 1)] * wide, axis=0, keepdims=True) for k in range(len(tables))
    ]


def split(x):
    high = x.astype(bf16)
    return high, (x - high.astype(f32)).astype(bf16)


def filter_kernel(
    doms, bounds, scale, x_ref, stiff_ref, pot_ref, conn_ref, faces_ref,
    out_ref, weight_ref, first_ref,
    oa, ob, hot, a_mat, at_mat, qa_ref, qb_ref, wpot_ref, parts, rows, sums, local, field, send, recv,
    send_sem, recv_sem,
):
    d = lax.axis_index("dom")
    has_left = d > 0
    has_right = d < doms - 1
    barrier = pltpu.get_barrier_semaphore()

    for peer in (lax.rem(d + doms - 1, doms), lax.rem(d + 1, doms)):
        pl.semaphore_signal(barrier, inc=1, device_id={"dom": peer}, device_id_type=MESH_ID)

    conn = conn_ref[...]
    faces = faces_ref[...]
    oa[...] = one_hot_rows(lax.shift_right_logical(conn, 5), 128)
    ob[...] = one_hot_rows(lax.bitwise_and(conn, 31), 32)
    hi_tab, lo_tab, count, seen = node_tables(conn, faces, oa, ob)
    pot = pot_ref[...]
    pot_hi = pot.astype(bf16).astype(f32)
    pot_mid = (pot - pot_hi).astype(bf16).astype(f32)
    pot_lo = pot - pot_hi - pot_mid
    for c in range(CELLS):
        part = slice(c * NPC, (c + 1) * NPC)
        qa, qb, cnt, p0, p1, p2, prior = at_entries(
            [hi_tab, lo_tab, count, pot_hi, pot_mid, pot_lo, seen[c]], oa[:, part], ob[:, part]
        )
        qa_ref[:, part] = qa.astype(jnp.int32)
        qb_ref[:, part] = qb.astype(jnp.int32)
        wpot_ref[:, part] = (p0 + p1 + p2) / cnt
        is_first = prior < 0.5
        on_left = (qa >= 0.0) & (qa * 128.0 + qb < SH) & has_left
        weight_ref[:, part] = jnp.where(is_first & jnp.logical_not(on_left), 1.0, 0.0)
        first_ref[:, part] = jnp.where(is_first, conn[:, part], -1)

    low_hot = one_hot_rows(lax.bitwise_and(conn, 127), 128)
    block = lax.shift_right_logical(conn, 7)
    chunk = 4
    for g in range(LNP // 128 // chunk):
        for k in range(chunk):
            mine = jnp.where(block == g * chunk + k, 1.0, 0.0).astype(bf16)
            hot[k * 128 : (k + 1) * 128] = low_hot * mine
        term = dot(x_ref[:, g * chunk * 128 : (g + 1) * chunk * 128], hot[...])
        local[...] = term if g == 0 else local[...] + term
    for c in range(CELLS):
        field[0, c * 64 : (c + 1) * 64] = local[:, c * NPC : (c + 1) * NPC].astype(bf16)

    qb_hot = one_hot_rows(qb_ref[...], 128)
    for j in range(SPEC // 128):
        mine = jnp.where(qa_ref[...] == j, 1.0, 0.0).astype(bf16)
        at_mat[j * 128 : (j + 1) * 128] = qb_hot * mine
    lane = lax.broadcasted_iota(jnp.int32, (128, 128), 1)

    @pl.loop(0, ENT // 128)
    def _(i):
        part = pl.ds(pl.multiple_of(i * 128, 128), 128)
        qa_col = as_column(qa_ref[:, part])
        qb_col = jnp.where(as_column(qb_ref[:, part]) == lane, 1.0, 0.0).astype(bf16)
        for j in range(SPEC // 128):
            mine = jnp.where(qa_col == j, 1.0, 0.0).astype(bf16)
            a_mat[part, j * 128 : (j + 1) * 128] = qb_col * mine

    pl.semaphore_wait(barrier, 2)

    center = (bounds[1] + bounds[0]) / 2.0
    half_width = (bounds[1] - bounds[0]) / 2.0
    in_face = lax.broadcasted_iota(jnp.int32, (1, FACE), 1) < SH
    for step in range(DEGREE):
        old = field.at[(step + 1) % 2]
        now = field.at[step % 2]
        products = dot(now[...], stiff_ref[...])
        for c in range(CELLS):
            part = slice(c * NPC, (c + 1) * NPC)
            block_rows = slice(c * 64, (c + 1) * 64)
            value = products[block_rows] * scale[c] + wpot_ref[:, part] * now[block_rows].astype(f32)
            local[:, part] = value
            high, low = split(value)
            parts[0:64, part] = high
            parts[64:128, part] = low
        both = dot(parts[...], a_mat[:, 0 : 2 * FACE])
        sums[:, 0 : 2 * FACE] = both[0:64] + both[64:128]
        send[step, 0] = sums[:, 0:FACE].astype(bf16)
        send[step, 1] = sums[:, FACE : 2 * FACE].astype(bf16)
        down = pltpu.make_async_remote_copy(
            src_ref=send.at[step, 0], dst_ref=recv.at[step, 1],
            send_sem=send_sem.at[step, 0], recv_sem=recv_sem.at[step, 1],
            device_id={"dom": d - 1}, device_id_type=MESH_ID)
        up = pltpu.make_async_remote_copy(
            src_ref=send.at[step, 1], dst_ref=recv.at[step, 0],
            send_sem=send_sem.at[step, 1], recv_sem=recv_sem.at[step, 0],
            device_id={"dom": d + 1}, device_id_type=MESH_ID)

        @pl.when(has_left)
        def _():
            down.start()

        @pl.when(has_right)
        def _():
            up.start()

        both = dot(parts[...], a_mat[:, 2 * FACE : SPEC])
        high, low = split(both[0:64] + both[64:128])
        rows[0:64, 2 * FACE : SPEC] = high
        rows[64:128, 2 * FACE : SPEC] = low
        spread = dot(rows[:, 2 * FACE : SPEC], at_mat[2 * FACE : SPEC])

        @pl.when(has_left)
        def _():
            down.wait_send()
            up.wait_recv()

        @pl.when(has_right)
        def _():
            up.wait_send()
            down.wait_recv()

        for side, there in ((0, has_left), (1, has_right)):
            part = slice(side * FACE, (side + 1) * FACE)
            came = jnp.where(in_face & there, recv[step, side].astype(f32), 0.0)
            high, low = split(sums[:, part] + came)
            rows[0:64, part] = high
            rows[64:128, part] = low
        spread = spread + dot(rows[:, 0 : 2 * FACE], at_mat[0 : 2 * FACE])
        spread = spread[0:64] + spread[64:128]
        for c in range(CELLS):
            part = slice(c * NPC, (c + 1) * NPC)
            block_rows = slice(c * 64, (c + 1) * 64)
            h = jnp.where(qa_ref[:, part] >= 0, spread[:, part], local[:, part])
            fresh = (h - center * now[block_rows].astype(f32)) / half_width
            if step > 0:
                fresh = 2.0 * fresh - old[block_rows].astype(f32)
            if step == DEGREE - 1:
                out_ref[block_rows] = fresh.astype(bf16)
            else:
                old[block_rows] = fresh.astype(bf16)


def filtered(start_states, stiffness, cell_scale, potential, connectivity, shared_nodes, filter_bounds, doms):
    pot_tab = jnp.pad(potential, (0, 128 * 32 - LNP)).reshape(128, 32)
    conn = connectivity.reshape(1, ENT)
    faces = jnp.pad(shared_nodes[0], ((0, 0), (0, FACE - SH)), constant_values=-1)
    vmem = pl.BlockSpec(memory_space=pltpu.VMEM)
    smem = pl.BlockSpec(memory_space=pltpu.SMEM)
    return pl.pallas_call(
        functools.partial(filter_kernel, doms),
        out_shape=(
            jax.ShapeDtypeStruct((512, NPC), bf16),
            jax.ShapeDtypeStruct((1, ENT), f32),
            jax.ShapeDtypeStruct((1, ENT), jnp.int32),
        ),
        in_specs=[smem, smem] + [vmem] * 5,
        out_specs=(vmem, vmem, vmem),
        scratch_shapes=[
            pltpu.VMEM((128, ENT), bf16),
            pltpu.VMEM((32, ENT), bf16),
            pltpu.VMEM((512, ENT), bf16),
            pltpu.VMEM((ENT, SPEC), bf16),
            pltpu.VMEM((SPEC, ENT), bf16),
            pltpu.VMEM((1, ENT), jnp.int32),
            pltpu.VMEM((1, ENT), jnp.int32),
            pltpu.VMEM((1, ENT), f32),
            pltpu.VMEM((128, ENT), bf16),
            pltpu.VMEM((128, SPEC), bf16),
            pltpu.VMEM((64, 2 * FACE), f32),
            pltpu.VMEM((64, ENT), f32),
            pltpu.VMEM((2, 512, NPC), bf16),
            pltpu.VMEM((DEGREE, 2, 64, FACE), bf16),
            pltpu.VMEM((DEGREE, 2, 64, FACE), bf16),
            pltpu.SemaphoreType.DMA((DEGREE, 2)),
            pltpu.SemaphoreType.DMA((DEGREE, 2)),
        ],
        compiler_params=pltpu.CompilerParams(
            collective_id=0, has_side_effects=True, vmem_limit_bytes=56 << 20),
        name="filter",
    )(filter_bounds, cell_scale, start_states, stiffness, pot_tab, conn, faces)


def to_nodes_kernel(x_ref, first_ref, out_ref, hot, acc):
    lane = lax.broadcasted_iota(jnp.int32, (128, 128), 1)
    for c in range(CELLS):

        @pl.loop(0, NPC // 128)
        def _(i):
            at = pl.ds(pl.multiple_of(c * NPC + i * 128, 128), 128)
            here = pl.ds(pl.multiple_of(i * 128, 128), 128)
            node = as_column(first_ref[:, at])
            low = jnp.where(lax.bitwise_and(node, 127) == lane, 1.0, 0.0).astype(bf16)
            block = lax.shift_right_arithmetic(node, 7)
            for j in range(LNP // 128):
                mine = jnp.where(block == j, 1.0, 0.0).astype(bf16)
                hot[here, j * 128 : (j + 1) * 128] = low * mine

        term = dot(x_ref[c * 64 : (c + 1) * 64], hot[...])
        acc[...] = term if c == 0 else acc[...] + term
    out_ref[...] = acc[...].astype(bf16)


def to_nodes(x, first):
    vmem = pl.BlockSpec(memory_space=pltpu.VMEM)
    return pl.pallas_call(
        to_nodes_kernel,
        out_shape=jax.ShapeDtypeStruct((64, LNP), bf16),
        in_specs=[vmem, vmem],
        out_specs=vmem,
        scratch_shapes=[pltpu.VMEM((NPC, LNP), bf16), pltpu.VMEM((64, LNP), f32)],
        compiler_params=pltpu.CompilerParams(vmem_limit_bytes=40 << 20),
        name="to_nodes",
    )(x, first)


def inverse_root(gram):
    frobenius = jnp.sqrt(jnp.sum(gram * gram) + 1e-06)
    iterate = gram / frobenius
    identity = jnp.eye(gram.shape[0], dtype=f32)
    inverse = identity
    for sweep in range(NS_ITERS):
        factor = 1.5 * identity - 0.5 * jnp.dot(inverse, iterate, precision=lax.Precision.HIGHEST)
        iterate = jnp.dot(iterate, factor, precision=lax.Precision.HIGHEST)
        inverse = jnp.dot(factor, inverse, precision=lax.Precision.HIGHEST)
    return (inverse / jnp.sqrt(frobenius)).astype(bf16)


def exchange(x):
    blocks = x.reshape(CELLS, 64, NPC)
    return lax.all_to_all(blocks, "st", split_axis=0, concat_axis=0, tiled=True).reshape(512, NPC)


def body(doms, start_states, stiffness, cell_scale, potential, connectivity, shared_nodes, filter_bounds):
    states, weight, first = filtered(
        start_states, stiffness, cell_scale, potential, connectivity, shared_nodes, filter_bounds, doms)
    mine = lax.dynamic_slice_in_dim(weight, lax.axis_index("st") * NPC, NPC, 1)
    cell = exchange(states)
    partial = contract_last((cell.astype(f32) * mine).astype(bf16), cell)
    gram = lax.psum(partial, ("dom", "st"))
    coeffs = inverse_root(gram)
    rotated = lax.dot_general(coeffs, cell, (((0,), (0,)), ((), ())), preferred_element_type=f32).astype(bf16)
    return to_nodes(exchange(rotated), first)


def solution(mesh):
    in_specs = (P("st", "dom"), P(), P("dom"), P("dom"), P("dom", None), P("dom", None, None), P())
    return jax.shard_map(
        functools.partial(body, mesh.shape["dom"]), mesh=mesh, in_specs=in_specs, out_specs=P("st", "dom"),
        check_vma=False)
```

profile of v0, /device:TPU:1, one launch (start us, length us, event | category | flops | bytes accessed | tf_op | source)
XLA Modules:
  0.0 392.3 jit_solution(12904653130447910438)
XLA Ops:
  6.5 0.0 copy-start.2
  6.5 1.3 copy.8
  7.9 0.0 copy-done.2
  7.9 0.0 copy-start.3
  7.9 0.7 reshape.24.pot_ref
  8.6 0.0 copy-done.3
  8.6 0.6 pad.9.faces_ref
  9.2 37.9 %filter.1 = (bf16[512,512]{1,0:T(8,128)(2,1)}, f32[1,4096]{1,0:T(1,128)}, s32[1,4096]{1,0:T(1,128)}) custom-call(f32[2]{0:T(128)} %bounds.1, f32[8]{0:T(128)} %scale.1, bf16[64,3584]{1,0:T(8,128)(2,1)} %x_ref.1, bf16[512,512]{1,0:T(8,128)(2,1)} %stiff_ref.1, f32[128,32]{1,0:T(8,128)} %reshape.24.pot_ref, s32[1,4096]{1,0:T(1,128)} %bitcast.32, ...), custom_call_target="tpu_custom_call" | custom-call | tf_op jit(solution)/shard_map/filter/pallas_call | solution.py:234
  47.2 10.6 %all-to-all-start = ((bf16[8,64,512]{2,1,0:T(8,128)(2,1)}), bf16[8,64,512]{2,1,0:T(8,128)(2,1)S(1)}, u32[]{:S(2)}, u32[]{:S(2)}) async-start(bf16[8,64,512]{2,1,0:T(8,128)(2,1)} %bitcast.30), calls=%async_computation | async-start | bytes 1048576 | tf_op jit(solution)/shard_map/all_to_all | solution.py:315
  57.8 0.2 all-reduce.4.cloned.1.call-start
  58.0 0.7 constant_dynamic-slice_fusion
  58.7 15.2 %all-to-all-done = bf16[8,64,512]{2,1,0:T(8,128)(2,1)S(1)} async-done(((bf16[8,64,512]{2,1,0:T(8,128)(2,1)}), bf16[8,64,512]{2,1,0:T(8,128)(2,1)S(1)}, u32[]{:S(2)}, u32[]{:S(2)}) %all-to-all-start) | async-done | bytes 524320 | tf_op jit(solution)/shard_map/all_to_all | solution.py:315
  73.9 0.1 multiply_convert_fusion
  74.0 1.5 fusion.3
  75.4 0.0 all-reduce.4.cloned.1.call-update
  75.5 253.2 %all-reduce.4.cloned.1.call-done = f32[512,512]{1,0:T(8,128)} async-done(((f32[512,512]{1,0:T(8,128)}), f32[512,512]{1,0:T(8,128)}) %all-reduce.4.cloned.1.call-update) | async-done | bytes 1048592 | tf_op jit(solution)/shard_map/psum | solution.py:324
  328.7 0.0 copy-start.1
  328.7 2.2 multiply_reduce_fusion
  331.6 0.0 copy-done.1
  331.6 1.1 select_subtract_fusion.2
  332.7 1.0 fusion.1
  333.7 1.9 fusion.2
  335.6 1.9 select_subtract_fusion.1
  337.4 1.8 fusion.4
  339.3 1.8 fusion.5
  341.1 1.9 select_subtract_fusion
  343.0 2.1 fusion
  345.1 0.5 convolution_convert_fusion
  345.6 0.0 copy-start
  345.6 22.3 %all_to_all.10 = bf16[8,64,512]{2,1,0:T(8,128)(2,1)S(1)} all-to-all(bf16[8,64,512]{2,1,0:T(8,128)(2,1)S(1)} %bitcast.31), channel_id=1, replica_groups=mesh['dom'=32,'st'=8] {'st'}, dimensions={0} | all-to-all | bytes 1048576 | tf_op jit(solution)/shard_map/all_to_all | solution.py:315
  367.8 0.0 copy-done
  367.8 17.4 %to_nodes.1 = bf16[64,3584]{1,0:T(8,128)(2,1)} custom-call(bf16[512,512]{1,0:T(8,128)(2,1)S(1)} %bitcast.26, s32[1,4096]{1,0:T(1,128)S(1)} %copy-done), custom_call_target="tpu_custom_call" | custom-call | tf_op jit(solution)/shard_map/to_nodes/pallas_call | solution.py:290
  (1 shorter events, 0.0 us)
Async XLA Ops:
  6.5 1.4 copy-start.2
  7.9 0.7 copy-start.3
  47.2 26.7 %all-to-all-start = ((bf16[8,64,512]{2,1,0:T(8,128)(2,1)}), bf16[8,64,512]{2,1,0:T(8,128)(2,1)S(1)}, u32[]{:S(2)}, u32[]{:S(2)}) async-start(bf16[8,64,512]{2,1,0:T(8,128)(2,1)} %bitcast.30), calls=%async_computation | async-start | bytes 1048576 | tf_op jit(solution)/shard_map/all_to_all | solution.py:315
  57.8 270.9 %all-reduce.4.cloned.1.call-start = ((), (), s32[]{:S(2)}) async-start(), calls=%async_computation.2 | async-start | bytes 2097152 | tf_op jit(solution)/shard_map/psum | solution.py:324
  328.7 2.9 copy-start.1
  345.6 22.3 %copy-start = (s32[1,4096]{1,0:T(1,128)S(1)}, s32[1,4096]{1,0:T(1,128)}, u32[]{:S(2)}) copy-start(s32[1,4096]{1,0:T(1,128)} %get-tuple-element.10.first_ref) | copy-start | bytes 49156
Sparse Core Ops, SparseCore 0:
  75.6 253.0 all-reduce.3
where the time goes:
time: 399 us; the launch traced here: 392 us
  waiting for transfers between devices  268 us (67%)
  Pallas kernels  55.3 us (14%)
  blocking collectives  22.3 us (6%)
  matrix products  15.4 us (4%)
  between operations  14.5 us (4%)
  starting transfers between devices  10.9 us (3%)
    psum x1, waiting for transfers between devices, body(): gram = lax.psum(partial, ('dom', 'st'))  253 us
    pallas_call x1, Pallas kernels, filtered(): pl.pallas_call(functools.partial(filter_kernel, doms), out_shape=(jax.Sha...  37.9 us
    all_to_all x1, blocking collectives, exchange(): lax.all_to_all(blocks, 'st', split_axis=0, concat_axis=0, tiled=True)  22.3 us
    pallas_call x1, Pallas kernels, to_nodes(): pl.pallas_call(to_nodes_kernel, out_shape=jax.ShapeDtypeStruct((64, LNP),...  17.4 us
    all_to_all x1, waiting for transfers between devices, exchange(): lax.all_to_all(blocks, 'st', split_axis=0, concat_axis=0, tiled=True)  15.2 us
    all_to_all x1, starting transfers between devices, exchange(): lax.all_to_all(blocks, 'st', split_axis=0, concat_axis=0, tiled=True)  10.6 us
  transfers between devices with their start and end apart: 2, of which 2 were waited for; matrix products, arithmetic and copies ran while one was open for 0% of the time, Pallas kernels for 0%

commit v1 on v0

--- a/solution.py
+++ b/solution.py
@@ -9,7 +9,6 @@
 f32 = jnp.float32
 bf16 = jnp.bfloat16
 DEGREE = 3
-NS_ITERS = 3
 CELLS = 8
 NPC = 512
 ENT = CELLS * NPC
@@ -265,66 +264,262 @@
     )(filter_bounds, cell_scale, start_states, stiffness, pot_tab, conn, faces)
 
 
-def to_nodes_kernel(x_ref, first_ref, out_ref, hot, acc):
+def product(a, b):
+    a_hi, a_lo = split(a)
+    b_hi, b_lo = split(b)
+    return dot(a_hi, b_hi) + (dot(a_hi, b_lo) + dot(a_lo, b_hi))
+
+
+def finish_kernel(
+    mine_ref, weight_ref, first_ref, out_ref,
+    got, hot, sums, half, from_core, from_x, from_y, line, total, gram, root, turned, back, acc,
+    sent, came,
+):
+    d = lax.axis_index("dom")
+    s = lax.axis_index("st")
+    core, y, z_lo = lax.rem(d, 2), lax.rem(lax.div(d, 2), 4), lax.div(d, 8)
+    x, z_hi = lax.rem(s, 4), lax.div(s, 4)
+    z = z_hi * 4 + z_lo
+
+    def device(core=core, y=y, z_lo=z_lo, x=x, z_hi=z_hi):
+        return {"dom": (z_lo * 4 + y) * 2 + core, "st": z_hi * 4 + x}
+
+    def around(at, by, count):
+        return lax.rem(at + by, count)
+
+    def along_z(by):
+        there = around(z, by, 8)
+        return device(z_lo=lax.rem(there, 4), z_hi=lax.div(there, 4))
+
+    count = [0]
+
+    def copy(src, dst, to):
+        k = count[0]
+        count[0] += 1
+        return pltpu.make_async_remote_copy(
+            src_ref=src, dst_ref=dst, send_sem=sent.at[k], recv_sem=came.at[k], device_id=to, device_id_type=MESH_ID)
+
+    def start(copies):
+        for one in copies:
+            one.start()
+        return copies
+
+    def finish(copies):
+        for one in copies:
+            one.wait()
+
+    peers = [device(core=1 - core)]
+    peers += [device(y=around(y, k, 4)) for k in range(1, 4)]
+    peers += [along_z(k) for k in range(1, 8)]
+    peers += [device(x=around(x, k, 4)) for k in range(1, 4)]
+    peers += [device(x=around(x, k, 4), z_hi=1 - z_hi) for k in range(1, 4)]
+    barrier = pltpu.get_barrier_semaphore()
+    for peer in peers:
+        pl.semaphore_signal(barrier, inc=1, device_id=peer, device_id_type=MESH_ID)
+    pl.semaphore_wait(barrier, len(peers))
+
+    def pair_rows(at):
+        return pl.ds(pl.multiple_of(at * 128, 128), 128)
+
+    def cell_rows(at, k):
+        return pl.ds(pl.multiple_of(at * 128 + k * 64, 64), 64)
+
+    crossing = []
+    for k in range(4):
+        there = around(x, k, 4)
+        crossing.append(copy(
+            mine_ref.at[cell_rows(there, 1 - z_hi)], got.at[s, cell_rows(0, 1 - z_hi)],
+            device(x=there, z_hi=1 - z_hi)))
+    start(crossing)
+    beside = []
+    for k in range(1, 4):
+        there = around(x, k, 4)
+        beside.append(copy(mine_ref.at[pair_rows(there)], got.at[s], device(x=there)))
+    start(beside)
+    late = []
+    for k in range(4):
+        there = around(x, k, 4)
+        late.append(copy(
+            mine_ref.at[cell_rows(there, z_hi)], got.at[s, cell_rows(0, z_hi)],
+            device(x=there, z_hi=1 - z_hi)))
+    start(late)
+    got[s] = mine_ref[pair_rows(x)]
+
     lane = lax.broadcasted_iota(jnp.int32, (128, 128), 1)
-    for c in range(CELLS):
-
-        @pl.loop(0, NPC // 128)
-        def _(i):
-            at = pl.ds(pl.multiple_of(c * NPC + i * 128, 128), 128)
-            here = pl.ds(pl.multiple_of(i * 128, 128), 128)
-            node = as_column(first_ref[:, at])
-            low = jnp.where(lax.bitwise_and(node, 127) == lane, 1.0, 0.0).astype(bf16)
-            block = lax.shift_right_arithmetic(node, 7)
-            for j in range(LNP // 128):
-                mine = jnp.where(block == j, 1.0, 0.0).astype(bf16)
-                hot[here, j * 128 : (j + 1) * 128] = low * mine
-
-        term = dot(x_ref[c * 64 : (c + 1) * 64], hot[...])
-        acc[...] = term if c == 0 else acc[...] + term
-    out_ref[...] = acc[...].astype(bf16)
-
-
-def to_nodes(x, first):
+
+    @pl.loop(0, ENT // 128)
+    def _(i):
+        at = pl.ds(pl.multiple_of(i * 128, 128), 128)
+        node = as_column(first_ref[:, at])
+        low = jnp.where(lax.bitwise_and(node, 127) == lane, 1.0, 0.0).astype(bf16)
+        block = lax.shift_right_arithmetic(node, 7)
+        for j in range(LNP // 128):
+            mine = jnp.where(block == j, 1.0, 0.0).astype(bf16)
+            hot[at, j * 128 : (j + 1) * 128] = low * mine
+
+    finish(beside)
+    finish(crossing)
+
+    def weighted(rows, at):
+        mark = weight_ref[:, pl.ds(pl.multiple_of(at * NPC, NPC), NPC)]
+        return (rows.astype(f32) * mark).astype(bf16)
+
+    own = pl.ds(pl.multiple_of(z_hi * 4, 4), 4)
+    first_cell = got[own, 0:64].reshape(256, NPC)
+    second_cell = got[own, 64:128].reshape(256, NPC)
+    sums[0] = contract_last(weighted(first_cell, 2 * x), first_cell) + contract_last(
+        weighted(second_cell, 2 * x + 1), second_cell)
+    shared_rows = pl.ds(pl.multiple_of(z_hi * 64, 64), 64)
+    low_half = got[0:4, shared_rows].reshape(256, NPC)
+    high_half = got[4:8, shared_rows].reshape(256, NPC)
+    sums[1] = contract_last(weighted(low_half, 2 * x + z_hi), high_half)
+
+    half[0] = sums[0].astype(bf16)
+    half[1] = sums[1].astype(bf16)
+    finish(start([copy(half.at[1 - core], from_core, device(core=1 - core))]))
+    sums[core] = sums[core] + from_core[...].astype(f32)
+    half[core] = sums[core].astype(bf16)
+    finish(start([
+        copy(half.at[core, pl.ds(pl.multiple_of(around(x, k, 4) * 64, 64), 64)], from_x.at[k - 1],
+             device(x=around(x, k, 4)))
+        for k in range(1, 4)]))
+    quarter = sums[core, pl.ds(pl.multiple_of(x * 64, 64), 64)]
+    for k in range(3):
+        quarter = quarter + from_x[k].astype(f32)
+    sums[0, 0:64] = quarter
+    turned[0, 0:64, 0:256] = quarter.astype(bf16)
+    finish(start([
+        copy(turned.at[0, pl.ds(pl.multiple_of(around(y, k, 4) * 16, 16), 16), pl.ds(0, 256)], from_y.at[k - 1],
+             device(y=around(y, k, 4)))
+        for k in range(1, 4)]))
+    piece = sums[0, pl.ds(pl.multiple_of(y * 16, 16), 16)]
+    for k in range(3):
+        piece = piece + from_y[k].astype(f32)
+    line[z] = piece.astype(bf16)
+    finish(start([copy(line.at[z], line.at[z], along_z(k)) for k in range(1, 8)]))
+    low_sum = line[0].astype(f32)
+    high_sum = line[4].astype(f32)
+    for k in range(1, 4):
+        low_sum = low_sum + line[k].astype(f32)
+        high_sum = high_sum + line[4 + k].astype(f32)
+    on_core = 2 * core
+    piece_rows = pl.ds(pl.multiple_of(x * 64 + y * 16, 16), 16)
+
+    @pl.when(core == 0)
+    def _():
+        total[1, piece_rows] = high_sum.astype(bf16)
+
+    total[on_core, piece_rows] = (low_sum + jnp.where(core == 1, high_sum, 0.0)).astype(bf16)
+
+    def spread(rows, to):
+        first = [copy(total.at[on_core, rows], total.at[on_core, rows], one) for one in to]
+        second = [copy(total.at[1, rows], total.at[1, rows], one) for one in to]
+        start(first)
+
+        @pl.when(core == 0)
+        def _():
+            start(second)
+
+        finish(first)
+
+        @pl.when(core == 0)
+        def _():
+            finish(second)
+
+    spread(piece_rows, [device(y=around(y, k, 4)) for k in range(1, 4)])
+    spread(pl.ds(pl.multiple_of(x * 64, 64), 64), [device(x=around(x, k, 4)) for k in range(1, 4)])
+    down = [copy(total.at[k], total.at[k], device(core=1 - core)) for k in range(3)]
+
+    @pl.when(core == 0)
+    def _():
+        start(down[0:2])
+        for one in down[0:2]:
+            one.wait_send()
+        down[2].wait_recv()
+
+    @pl.when(core == 1)
+    def _():
+        start(down[2:3])
+        down[2].wait_send()
+        for one in down[0:2]:
+            one.wait_recv()
+
+    upper = total[2].astype(f32)
+    gram[0:256, 0:256] = total[0].astype(f32)
+    gram[256:512, 256:512] = total[1].astype(f32)
+    gram[0:256, 256:512] = upper
+    gram[256:512, 0:256] = jnp.transpose(upper)
+    g = gram[...]
+    frobenius = jnp.sqrt(jnp.sum(jnp.sum(g * g, axis=1, keepdims=True), axis=0, keepdims=True) + 1e-06)
+    a = g / frobenius
+    gram[...] = a
+    square = product(a, a)
+    diagonal = lax.broadcasted_iota(jnp.int32, (512, 512), 0) == lax.broadcasted_iota(jnp.int32, (512, 512), 1)
+    root[...] = (
+        jnp.where(diagonal, 2.25, 0.0) - 2.4375 * a + 1.6875 * square
+        + product(square, 0.0625 * square - 0.5625 * a))
+    columns = root[:, pl.ds(pl.multiple_of(z_hi * 256, 256), 256)]
+    cubed = product(root[...], product(root[...], columns))
+    coeffs = ((1.5 * columns - 0.5 * product(gram[...], cubed)) / jnp.sqrt(frobenius)).astype(bf16)
+
+    finish(late)
+    for k in range(2):
+        cell = got[:, k * 64 : (k + 1) * 64].reshape(512, NPC)
+        rotated = lax.dot_general(coeffs, cell, (((0,), (0,)), ((), ())), preferred_element_type=f32)
+        turned[:, k * 64 : (k + 1) * 64] = rotated.astype(bf16).reshape(4, 64, NPC)
+    returned = start([
+        copy(turned.at[around(x, k, 4)], back.at[x], device(x=around(x, k, 4))) for k in range(1, 4)])
+    back[x] = turned[x]
+    for k in range(4):
+        source = around(x, 4 - k, 4)
+        if k:
+            returned[k - 1].wait()
+        pair = jnp.concatenate([back[source, 0:64], back[source, 64:128]], axis=1)
+        term = dot(pair, hot[pl.ds(pl.multiple_of(source * 1024, 1024), 1024)])
+        if k == 0:
+            acc[...] = term
+        elif k < 3:
+            acc[...] = acc[...] + term
+        else:
+            out_ref[...] = (acc[...] + term).astype(bf16)
+
+
+def finished(states, weight, first):
     vmem = pl.BlockSpec(memory_space=pltpu.VMEM)
+    copies = 11 + 1 + 3 + 3 + 7 + 12 + 3 + 3
     return pl.pallas_call(
-        to_nodes_kernel,
+        finish_kernel,
         out_shape=jax.ShapeDtypeStruct((64, LNP), bf16),
-        in_specs=[vmem, vmem],
+        in_specs=[vmem] * 3,
         out_specs=vmem,
-        scratch_shapes=[pltpu.VMEM((NPC, LNP), bf16), pltpu.VMEM((64, LNP), f32)],
-        compiler_params=pltpu.CompilerParams(vmem_limit_bytes=40 << 20),
-        name="to_nodes",
-    )(x, first)
-
-
-def inverse_root(gram):
-    frobenius = jnp.sqrt(jnp.sum(gram * gram) + 1e-06)
-    iterate = gram / frobenius
-    identity = jnp.eye(gram.shape[0], dtype=f32)
-    inverse = identity
-    for sweep in range(NS_ITERS):
-        factor = 1.5 * identity - 0.5 * jnp.dot(inverse, iterate, precision=lax.Precision.HIGHEST)
-        iterate = jnp.dot(iterate, factor, precision=lax.Precision.HIGHEST)
-        inverse = jnp.dot(factor, inverse, precision=lax.Precision.HIGHEST)
-    return (inverse / jnp.sqrt(frobenius)).astype(bf16)
-
-
-def exchange(x):
-    blocks = x.reshape(CELLS, 64, NPC)
-    return lax.all_to_all(blocks, "st", split_axis=0, concat_axis=0, tiled=True).reshape(512, NPC)
+        scratch_shapes=[
+            pltpu.VMEM((8, 128, NPC), bf16),
+            pltpu.VMEM((ENT, LNP), bf16),
+            pltpu.VMEM((2, 256, 256), f32),
+            pltpu.VMEM((2, 256, 256), bf16),
+            pltpu.VMEM((256, 256), bf16),
+            pltpu.VMEM((3, 64, 256), bf16),
+            pltpu.VMEM((3, 16, 256), bf16),
+            pltpu.VMEM((8, 16, 256), bf16),
+            pltpu.VMEM((3, 256, 256), bf16),
+            pltpu.VMEM((512, 512), f32),
+            pltpu.VMEM((512, 512), f32),
+            pltpu.VMEM((4, 128, NPC), bf16),
+            pltpu.VMEM((4, 128, NPC), bf16),
+            pltpu.VMEM((64, LNP), f32),
+            pltpu.SemaphoreType.DMA((copies,)),
+            pltpu.SemaphoreType.DMA((copies,)),
+        ],
+        compiler_params=pltpu.CompilerParams(
+            collective_id=1, has_side_effects=True, vmem_limit_bytes=56 << 20),
+        name="finish",
+    )(states, weight, first)
 
 
 def body(doms, start_states, stiffness, cell_scale, potential, connectivity, shared_nodes, filter_bounds):
     states, weight, first = filtered(
         start_states, stiffness, cell_scale, potential, connectivity, shared_nodes, filter_bounds, doms)
-    mine = lax.dynamic_slice_in_dim(weight, lax.axis_index("st") * NPC, NPC, 1)
-    cell = exchange(states)
-    partial = contract_last((cell.astype(f32) * mine).astype(bf16), cell)
-    gram = lax.psum(partial, ("dom", "st"))
-    coeffs = inverse_root(gram)
-    rotated = lax.dot_general(coeffs, cell, (((0,), (0,)), ((), ())), preferred_element_type=f32).astype(bf16)
-    return to_nodes(exchange(rotated), first)
+    return finished(states, weight, first)
 
 
 def solution(mesh):

time: 399 us -> 119 us (0.30); the launches traced: 392 us -> 119 us
  waiting for transfers between devices: 268 us -> 0 us
  Pallas kernels: 55.3 us -> 113 us
  blocking collectives: 22.3 us -> 0 us
  matrix products: 15.4 us -> 0 us
  between operations: 14.5 us -> 0.02 us
  starting transfers between devices: 10.9 us -> 0 us
    psum x1 -> x0, waiting for transfers between devices: 253 us -> none  [body(): gram = lax.psum(partial, ('dom', 'st'))]
    pallas_call x1, Pallas kernels: 17.4 us -> 75.7 us  [finished(): pl.pallas_call(finish_kernel, out_shape=jax.ShapeDtypeStruct((64, LNP), b...]
    all_to_all x1 -> x0, blocking collectives: 22.3 us -> none  [exchange(): lax.all_to_all(blocks, 'st', split_axis=0, concat_axis=0, tiled=True)]
    dot_general x10 -> x0, matrix products: 15.4 us -> none  [the longest x3 4.9 us: inverse_root(): inverse = jnp.dot(factor, inverse, precision=lax.Precision.HIGHEST)]
    all_to_all x1 -> x0, waiting for transfers between devices: 15.2 us -> none  [exchange(): lax.all_to_all(blocks, 'st', split_axis=0, concat_axis=0, tiled=True)]
    all_to_all x1 -> x0, starting transfers between devices: 10.6 us -> none  [exchange(): lax.all_to_all(blocks, 'st', split_axis=0, concat_axis=0, tiled=True)]
  transfers between devices with their start and end apart: 2 -> 0, of which waited for: 2 -> 0; matrix products, arithmetic and copies ran while one was open for 0% -> 0% of each run, Pallas kernels for 0% -> 0%
where the time goes in v1:
time: 119 us
  Pallas kernels  113 us (95%)
  local copies, waits for them, and re-layouts  5.17 us (4%)
    pallas_call x1, Pallas kernels, finished(): pl.pallas_call(finish_kernel, out_shape=jax.ShapeDtypeStruct((64, LNP), b...  75.7 us
    pallas_call x1, Pallas kernels, filtered(): pl.pallas_call(functools.partial(filter_kernel, doms), out_shape=(jax.Sha...  37.6 us
    unnamed x4, local copies, waits for them, and re-layouts  2.44 us

profile of v1, /device:TPU:1, one launch (start us, length us, event | category | flops | bytes accessed | tf_op | source)
XLA Modules:
  0.0 118.6 jit_solution(8722133482554299847)
XLA Ops:
  0.0 1.3 %pad.9.faces_ref = s32[2,512]{1,0:T(2,128)} pad(s32[2,435]{1,0:T(2,128)} %bitcast.6, s32[]{:T(128)} %constant.4.clone.1), padding=0_0x0_77 | pad | bytes 7580 | tf_op jit(solution)/shard_map/jit(_pad)/pad | solution.py:230
  1.3 0.0 copy-start
  1.3 0.7 pad.8
  2.0 0.0 copy-done
  2.0 0.6 copy.8
  2.6 0.7 reshape.6.pot_ref
  3.4 37.6 %filter.1 = (bf16[512,512]{1,0:T(8,128)(2,1)}, f32[1,4096]{1,0:T(1,128)}, s32[1,4096]{1,0:T(1,128)}) custom-call(f32[2]{0:T(128)} %bounds.1, f32[8]{0:T(128)} %scale.1, bf16[64,3584]{1,0:T(8,128)(2,1)} %x_ref.1, bf16[512,512]{1,0:T(8,128)(2,1)} %stiff_ref.1, f32[128,32]{1,0:T(8,128)} %reshape.6.pot_ref, s32[1,4096]{1,0:T(1,128)} %bitcast.4, ...), custom_call_target="tpu_custom_call" | custom-call | tf_op jit(solution)/shard_map/filter/pallas_call | solution.py:233
  41.0 75.7 %finish.1 = bf16[64,3584]{1,0:T(8,128)(2,1)} custom-call(bf16[512,512]{1,0:T(8,128)(2,1)} %get-tuple-element.8.mine_ref, f32[1,4096]{1,0:T(1,128)} %get-tuple-element.9.weight_ref, s32[1,4096]{1,0:T(1,128)} %get-tuple-element.10.first_ref), custom_call_target="tpu_custom_call" | custom-call | tf_op jit(solution)/shard_map/finish/pallas_call | solution.py:490
  116.8 1.8 %copy.10 = bf16[64,3584]{1,0:T(8,128)(2,1)} copy(bf16[64,3584]{1,0:T(8,128)(2,1)} %finish.1) | data formatting | bytes 917504
Async XLA Ops:
  1.3 0.7 copy-start

commit v2 on v1

--- a/solution.py
+++ b/solution.py
@@ -37,7 +37,7 @@
     return jnp.dot(a, b, preferred_element_type=f32)
 
 
-def node_tables(conn, faces, oa, ob):
+def node_tables(faces, oa, ob):
     total = jnp.zeros((128, 32), f32)
     seen = []
     for c in range(CELLS):
@@ -89,7 +89,7 @@
 def filter_kernel(
     doms, bounds, scale, x_ref, stiff_ref, pot_ref, conn_ref, faces_ref,
     out_ref, weight_ref, first_ref,
-    oa, ob, hot, a_mat, at_mat, qa_ref, qb_ref, wpot_ref, parts, rows, sums, local, field, send, recv,
+    nodes, faces, pot_rows, pot_tab, oa, ob, hot, a_mat, at_mat, qa_ref, qb_ref, wpot_ref, parts, rows, sums, local, field, send, recv,
     send_sem, recv_sem,
 ):
     d = lax.axis_index("dom")
@@ -100,12 +100,20 @@
     for peer in (lax.rem(d + doms - 1, doms), lax.rem(d + 1, doms)):
         pl.semaphore_signal(barrier, inc=1, device_id={"dom": peer}, device_id_type=MESH_ID)
 
-    conn = conn_ref[...]
-    faces = faces_ref[...]
+    for c in range(CELLS):
+        nodes[:, c * NPC : (c + 1) * NPC] = conn_ref[c : c + 1]
+    faces[...] = jnp.full((2, FACE), -1, jnp.int32)
+    faces[:, 0:SH] = faces_ref[0]
+    pot_rows[...] = jnp.zeros((32, 128), f32)
+    for k in range(LNP // 128):
+        pot_rows[k : k + 1] = pot_ref[pl.ds(k * 128, 128)].reshape(1, 128)
+    for k in range(4):
+        pot_tab[pl.ds(k, 32, stride=4)] = pot_rows[:, k * 32 : (k + 1) * 32]
+    conn = nodes[...]
     oa[...] = one_hot_rows(lax.shift_right_logical(conn, 5), 128)
     ob[...] = one_hot_rows(lax.bitwise_and(conn, 31), 32)
-    hi_tab, lo_tab, count, seen = node_tables(conn, faces, oa, ob)
-    pot = pot_ref[...]
+    hi_tab, lo_tab, count, seen = node_tables(faces[...], oa, ob)
+    pot = pot_tab[...]
     pot_hi = pot.astype(bf16).astype(f32)
     pot_mid = (pot - pot_hi).astype(bf16).astype(f32)
     pot_lo = pot - pot_hi - pot_mid
@@ -225,9 +233,6 @@
 
 
 def filtered(start_states, stiffness, cell_scale, potential, connectivity, shared_nodes, filter_bounds, doms):
-    pot_tab = jnp.pad(potential, (0, 128 * 32 - LNP)).reshape(128, 32)
-    conn = connectivity.reshape(1, ENT)
-    faces = jnp.pad(shared_nodes[0], ((0, 0), (0, FACE - SH)), constant_values=-1)
     vmem = pl.BlockSpec(memory_space=pltpu.VMEM)
     smem = pl.BlockSpec(memory_space=pltpu.SMEM)
     return pl.pallas_call(
@@ -240,6 +245,10 @@
         in_specs=[smem, smem] + [vmem] * 5,
         out_specs=(vmem, vmem, vmem),
         scratch_shapes=[
+            pltpu.VMEM((1, ENT), jnp.int32),
+            pltpu.VMEM((2, FACE), jnp.int32),
+            pltpu.VMEM((32, 128), f32),
+            pltpu.VMEM((128, 32), f32),
             pltpu.VMEM((128, ENT), bf16),
             pltpu.VMEM((32, ENT), bf16),
             pltpu.VMEM((512, ENT), bf16),
@@ -261,7 +270,7 @@
         compiler_params=pltpu.CompilerParams(
             collective_id=0, has_side_effects=True, vmem_limit_bytes=56 << 20),
         name="filter",
-    )(filter_bounds, cell_scale, start_states, stiffness, pot_tab, conn, faces)
+    )(filter_bounds, cell_scale, start_states, stiffness, potential, connectivity, shared_nodes)
 
 
 def product(a, b):
@@ -272,7 +281,7 @@
 
 def finish_kernel(
     mine_ref, weight_ref, first_ref, out_ref,
-    got, hot, sums, half, from_core, from_x, from_y, line, total, gram, root, turned, back, acc,
+    got, hot, sums, half, from_core, from_plane, line, total, gram, root, turned, back, acc,
     sent, came,
 ):
     d = lax.axis_index("dom")
@@ -309,9 +318,9 @@
             one.wait()
 
     peers = [device(core=1 - core)]
-    peers += [device(y=around(y, k, 4)) for k in range(1, 4)]
+    peers += [
+        device(x=around(x, kx, 4), y=around(y, ky, 4)) for kx in range(4) for ky in range(4) if kx + ky]
     peers += [along_z(k) for k in range(1, 8)]
-    peers += [device(x=around(x, k, 4)) for k in range(1, 4)]
     peers += [device(x=around(x, k, 4), z_hi=1 - z_hi) for k in range(1, 4)]
     barrier = pltpu.get_barrier_semaphore()
     for peer in peers:
@@ -342,7 +351,6 @@
         late.append(copy(
             mine_ref.at[cell_rows(there, z_hi)], got.at[s, cell_rows(0, z_hi)],
             device(x=there, z_hi=1 - z_hi)))
-    start(late)
     got[s] = mine_ref[pair_rows(x)]
 
     lane = lax.broadcasted_iota(jnp.int32, (128, 128), 1)
@@ -357,8 +365,9 @@
             mine = jnp.where(block == j, 1.0, 0.0).astype(bf16)
             hot[at, j * 128 : (j + 1) * 128] = low * mine
 
+    finish(crossing)
+    start(late[0:2])
     finish(beside)
-    finish(crossing)
 
     def weighted(rows, at):
         mark = weight_ref[:, pl.ds(pl.multiple_of(at * NPC, NPC), NPC)]
@@ -379,55 +388,47 @@
     finish(start([copy(half.at[1 - core], from_core, device(core=1 - core))]))
     sums[core] = sums[core] + from_core[...].astype(f32)
     half[core] = sums[core].astype(bf16)
+    plane = [(kx, ky) for kx in range(4) for ky in range(4)][1:]
+
+    def piece_of(kx, ky):
+        return pl.ds(pl.multiple_of(around(x, kx, 4) * 64 + around(y, ky, 4) * 16, 16), 16)
+
+    def in_plane(kx, ky):
+        return device(x=around(x, kx, 4), y=around(y, ky, 4))
+
     finish(start([
-        copy(half.at[core, pl.ds(pl.multiple_of(around(x, k, 4) * 64, 64), 64)], from_x.at[k - 1],
-             device(x=around(x, k, 4)))
-        for k in range(1, 4)]))
-    quarter = sums[core, pl.ds(pl.multiple_of(x * 64, 64), 64)]
-    for k in range(3):
-        quarter = quarter + from_x[k].astype(f32)
-    sums[0, 0:64] = quarter
-    turned[0, 0:64, 0:256] = quarter.astype(bf16)
-    finish(start([
-        copy(turned.at[0, pl.ds(pl.multiple_of(around(y, k, 4) * 16, 16), 16), pl.ds(0, 256)], from_y.at[k - 1],
-             device(y=around(y, k, 4)))
-        for k in range(1, 4)]))
-    piece = sums[0, pl.ds(pl.multiple_of(y * 16, 16), 16)]
-    for k in range(3):
-        piece = piece + from_y[k].astype(f32)
+        copy(half.at[core, piece_of(*by)], from_plane.at[k], in_plane(*by)) for k, by in enumerate(plane)]))
+    piece = sums[core, piece_of(0, 0)]
+    for k in range(15):
+        piece = piece + from_plane[k].astype(f32)
     line[z] = piece.astype(bf16)
     finish(start([copy(line.at[z], line.at[z], along_z(k)) for k in range(1, 8)]))
+    start(late[2:4])
     low_sum = line[0].astype(f32)
     high_sum = line[4].astype(f32)
     for k in range(1, 4):
         low_sum = low_sum + line[k].astype(f32)
         high_sum = high_sum + line[4 + k].astype(f32)
     on_core = 2 * core
-    piece_rows = pl.ds(pl.multiple_of(x * 64 + y * 16, 16), 16)
+    piece_rows = piece_of(0, 0)
 
     @pl.when(core == 0)
     def _():
         total[1, piece_rows] = high_sum.astype(bf16)
 
     total[on_core, piece_rows] = (low_sum + jnp.where(core == 1, high_sum, 0.0)).astype(bf16)
-
-    def spread(rows, to):
-        first = [copy(total.at[on_core, rows], total.at[on_core, rows], one) for one in to]
-        second = [copy(total.at[1, rows], total.at[1, rows], one) for one in to]
-        start(first)
-
-        @pl.when(core == 0)
-        def _():
-            start(second)
-
-        finish(first)
-
-        @pl.when(core == 0)
-        def _():
-            finish(second)
-
-    spread(piece_rows, [device(y=around(y, k, 4)) for k in range(1, 4)])
-    spread(pl.ds(pl.multiple_of(x * 64, 64), 64), [device(x=around(x, k, 4)) for k in range(1, 4)])
+    held = [copy(total.at[pl.ds(0, 2), piece_rows], total.at[pl.ds(0, 2), piece_rows], in_plane(*by)) for by in plane]
+    count[0] -= len(plane)
+    held_one = [copy(total.at[2, piece_rows], total.at[2, piece_rows], in_plane(*by)) for by in plane]
+
+    @pl.when(core == 0)
+    def _():
+        finish(start(held))
+
+    @pl.when(core == 1)
+    def _():
+        finish(start(held_one))
+
     down = [copy(total.at[k], total.at[k], device(core=1 - core)) for k in range(3)]
 
     @pl.when(core == 0)
@@ -486,7 +487,7 @@
 
 def finished(states, weight, first):
     vmem = pl.BlockSpec(memory_space=pltpu.VMEM)
-    copies = 11 + 1 + 3 + 3 + 7 + 12 + 3 + 3
+    copies = 11 + 1 + 15 + 7 + 15 + 3 + 3
     return pl.pallas_call(
         finish_kernel,
         out_shape=jax.ShapeDtypeStruct((64, LNP), bf16),
@@ -498,8 +499,7 @@
             pltpu.VMEM((2, 256, 256), f32),
             pltpu.VMEM((2, 256, 256), bf16),
             pltpu.VMEM((256, 256), bf16),
-            pltpu.VMEM((3, 64, 256), bf16),
-            pltpu.VMEM((3, 16, 256), bf16),
+            pltpu.VMEM((15, 16, 256), bf16),
             pltpu.VMEM((8, 16, 256), bf16),
             pltpu.VMEM((3, 256, 256), bf16),
             pltpu.VMEM((512, 512), f32),

time: 119 us -> 107 us (0.90)
  Pallas kernels: 113 us -> 105 us
  local copies, waits for them, and re-layouts: 5.17 us -> 1.82 us
    pallas_call x1, Pallas kernels: 75.7 us -> 66.9 us  [finished(): pl.pallas_call(finish_kernel, out_shape=jax.ShapeDtypeStruct((64, LNP), b...]
    pad x2 -> x0, local copies, waits for them, and re-layouts: 2.02 us -> none  [the longest x1 1.28 us: filtered(): jnp.pad(shared_nodes[0], ((0, 0), (0, FACE - SH)), constant_values=-1)]
    unnamed x4 -> x1, local copies, waits for them, and re-layouts: 2.44 us -> 1.82 us
where the time goes in v2:
time: 107 us; the launch traced here: 106 us
  Pallas kernels  105 us (98%)
  local copies, waits for them, and re-layouts  1.82 us (2%)
    pallas_call x1, Pallas kernels, finished(): pl.pallas_call(finish_kernel, out_shape=jax.ShapeDtypeStruct((64, LNP), b...  66.9 us
    pallas_call x1, Pallas kernels, filtered(): pl.pallas_call(functools.partial(filter_kernel, doms), out_shape=(jax.Sha...  37.7 us

profile of v2, /device:TPU:1, one launch (start us, length us, event | category | flops | bytes accessed | tf_op | source)
XLA Modules:
  0.0 106.4 jit_solution(7658739398014616265)
XLA Ops:
  0.0 37.7 %filter.1 = (bf16[512,512]{1,0:T(8,128)(2,1)}, f32[1,4096]{1,0:T(1,128)}, s32[1,4096]{1,0:T(1,128)}) custom-call(f32[2]{0:T(128)} %bounds.1, f32[8]{0:T(128)} %scale.1, bf16[64,3584]{1,0:T(8,128)(2,1)} %x_ref.1, bf16[512,512]{1,0:T(8,128)(2,1)} %stiff_ref.1, f32[3584]{0:T(1024)} %pot_ref.1, s32[8,512]{1,0:T(8,128)} %conn_ref.1, s32[1,2,435]{2,1,0:T(2,128)} %faces_ref.1), custom_call_target="tpu_custom_call" | custom-call | tf_op jit(solution)/shard_map/filter/pallas_call | solution.py:238
  37.7 66.9 %finish.1 = bf16[64,3584]{1,0:T(8,128)(2,1)} custom-call(bf16[512,512]{1,0:T(8,128)(2,1)} %get-tuple-element.8.mine_ref, f32[1,4096]{1,0:T(1,128)} %get-tuple-element.9.weight_ref, s32[1,4096]{1,0:T(1,128)} %get-tuple-element.10.first_ref), custom_call_target="tpu_custom_call" | custom-call | tf_op jit(solution)/shard_map/finish/pallas_call | solution.py:491
  104.6 1.8 %copy.9 = bf16[64,3584]{1,0:T(8,128)(2,1)} copy(bf16[64,3584]{1,0:T(8,128)(2,1)} %finish.1) | data formatting | bytes 917504

commit v3 on v2

--- a/solution.py
+++ b/solution.py
@@ -17,6 +17,7 @@
 SH = 435
 FACE = 512
 SPEC = 1536
+HALF = 2048
 MESH_ID = pl.DeviceIdType.MESH
 
 
@@ -86,20 +87,15 @@
     return high, (x - high.astype(f32)).astype(bf16)
 
 
-def filter_kernel(
-    doms, bounds, scale, x_ref, stiff_ref, pot_ref, conn_ref, faces_ref,
+def filter_states(
+    doms, wait_for_peers, bounds, scale, x_ref, stiff_ref, pot_ref, conn_ref, faces_ref,
     out_ref, weight_ref, first_ref,
-    nodes, faces, pot_rows, pot_tab, oa, ob, hot, a_mat, at_mat, qa_ref, qb_ref, wpot_ref, parts, rows, sums, local, field, send, recv,
-    send_sem, recv_sem,
+    big, nodes, faces, pot_rows, pot_tab, oa, ob, hot, qa_ref, qb_ref, wpot_ref, parts, rows, sums, local, spread, field,
+    send, recv, send_sem, recv_sem,
 ):
     d = lax.axis_index("dom")
     has_left = d > 0
     has_right = d < doms - 1
-    barrier = pltpu.get_barrier_semaphore()
-
-    for peer in (lax.rem(d + doms - 1, doms), lax.rem(d + 1, doms)):
-        pl.semaphore_signal(barrier, inc=1, device_id={"dom": peer}, device_id_type=MESH_ID)
-
     for c in range(CELLS):
         nodes[:, c * NPC : (c + 1) * NPC] = conn_ref[c : c + 1]
     faces[...] = jnp.full((2, FACE), -1, jnp.int32)
@@ -145,7 +141,9 @@
     qb_hot = one_hot_rows(qb_ref[...], 128)
     for j in range(SPEC // 128):
         mine = jnp.where(qa_ref[...] == j, 1.0, 0.0).astype(bf16)
-        at_mat[j * 128 : (j + 1) * 128] = qb_hot * mine
+        for h in range(2):
+            big[h * SPEC + j * 128 : h * SPEC + (j + 1) * 128, SPEC:LNP] = (
+                qb_hot[:, h * HALF : (h + 1) * HALF] * mine[:, h * HALF : (h + 1) * HALF])
     lane = lax.broadcasted_iota(jnp.int32, (128, 128), 1)
 
     @pl.loop(0, ENT // 128)
@@ -155,10 +153,9 @@
         qb_col = jnp.where(as_column(qb_ref[:, part]) == lane, 1.0, 0.0).astype(bf16)
         for j in range(SPEC // 128):
             mine = jnp.where(qa_col == j, 1.0, 0.0).astype(bf16)
-            a_mat[part, j * 128 : (j + 1) * 128] = qb_col * mine
-
-    pl.semaphore_wait(barrier, 2)
-
+            big[part, j * 128 : (j + 1) * 128] = qb_col * mine
+
+    wait_for_peers()
     center = (bounds[1] + bounds[0]) / 2.0
     half_width = (bounds[1] - bounds[0]) / 2.0
     in_face = lax.broadcasted_iota(jnp.int32, (1, FACE), 1) < SH
@@ -174,7 +171,7 @@
             high, low = split(value)
             parts[0:64, part] = high
             parts[64:128, part] = low
-        both = dot(parts[...], a_mat[:, 0 : 2 * FACE])
+        both = dot(parts[...], big[:, 0 : 2 * FACE])
         sums[:, 0 : 2 * FACE] = both[0:64] + both[64:128]
         send[step, 0] = sums[:, 0:FACE].astype(bf16)
         send[step, 1] = sums[:, FACE : 2 * FACE].astype(bf16)
@@ -195,11 +192,12 @@
         def _():
             up.start()
 
-        both = dot(parts[...], a_mat[:, 2 * FACE : SPEC])
+        both = dot(parts[...], big[:, 2 * FACE : SPEC])
         high, low = split(both[0:64] + both[64:128])
         rows[0:64, 2 * FACE : SPEC] = high
         rows[64:128, 2 * FACE : SPEC] = low
-        spread = dot(rows[:, 2 * FACE : SPEC], at_mat[2 * FACE : SPEC])
+        others = [
+            dot(rows[:, 2 * FACE : SPEC], big[h * SPEC + 2 * FACE : (h + 1) * SPEC, SPEC:LNP]) for h in range(2)]
 
         @pl.when(has_left)
         def _():
@@ -217,8 +215,9 @@
             high, low = split(sums[:, part] + came)
             rows[0:64, part] = high
             rows[64:128, part] = low
-        spread = spread + dot(rows[:, 0 : 2 * FACE], at_mat[0 : 2 * FACE])
-        spread = spread[0:64] + spread[64:128]
+        for h in range(2):
+            both = others[h] + dot(rows[:, 0 : 2 * FACE], big[h * SPEC : h * SPEC + 2 * FACE, SPEC:LNP])
+            spread[:, h * HALF : (h + 1) * HALF] = both[0:64] + both[64:128]
         for c in range(CELLS):
             part = slice(c * NPC, (c + 1) * NPC)
             block_rows = slice(c * 64, (c + 1) * 64)
@@ -232,58 +231,15 @@
                 old[block_rows] = fresh.astype(bf16)
 
 
-def filtered(start_states, stiffness, cell_scale, potential, connectivity, shared_nodes, filter_bounds, doms):
-    vmem = pl.BlockSpec(memory_space=pltpu.VMEM)
-    smem = pl.BlockSpec(memory_space=pltpu.SMEM)
-    return pl.pallas_call(
-        functools.partial(filter_kernel, doms),
-        out_shape=(
-            jax.ShapeDtypeStruct((512, NPC), bf16),
-            jax.ShapeDtypeStruct((1, ENT), f32),
-            jax.ShapeDtypeStruct((1, ENT), jnp.int32),
-        ),
-        in_specs=[smem, smem] + [vmem] * 5,
-        out_specs=(vmem, vmem, vmem),
-        scratch_shapes=[
-            pltpu.VMEM((1, ENT), jnp.int32),
-            pltpu.VMEM((2, FACE), jnp.int32),
-            pltpu.VMEM((32, 128), f32),
-            pltpu.VMEM((128, 32), f32),
-            pltpu.VMEM((128, ENT), bf16),
-            pltpu.VMEM((32, ENT), bf16),
-            pltpu.VMEM((512, ENT), bf16),
-            pltpu.VMEM((ENT, SPEC), bf16),
-            pltpu.VMEM((SPEC, ENT), bf16),
-            pltpu.VMEM((1, ENT), jnp.int32),
-            pltpu.VMEM((1, ENT), jnp.int32),
-            pltpu.VMEM((1, ENT), f32),
-            pltpu.VMEM((128, ENT), bf16),
-            pltpu.VMEM((128, SPEC), bf16),
-            pltpu.VMEM((64, 2 * FACE), f32),
-            pltpu.VMEM((64, ENT), f32),
-            pltpu.VMEM((2, 512, NPC), bf16),
-            pltpu.VMEM((DEGREE, 2, 64, FACE), bf16),
-            pltpu.VMEM((DEGREE, 2, 64, FACE), bf16),
-            pltpu.SemaphoreType.DMA((DEGREE, 2)),
-            pltpu.SemaphoreType.DMA((DEGREE, 2)),
-        ],
-        compiler_params=pltpu.CompilerParams(
-            collective_id=0, has_side_effects=True, vmem_limit_bytes=56 << 20),
-        name="filter",
-    )(filter_bounds, cell_scale, start_states, stiffness, potential, connectivity, shared_nodes)
-
-
 def product(a, b):
     a_hi, a_lo = split(a)
     b_hi, b_lo = split(b)
     return dot(a_hi, b_hi) + (dot(a_hi, b_lo) + dot(a_lo, b_hi))
 
 
-def finish_kernel(
-    mine_ref, weight_ref, first_ref, out_ref,
-    got, hot, sums, half, from_core, from_plane, line, total, gram, root, turned, back, acc,
-    sent, came,
-):
+def kernel(doms, bounds, scale, x_ref, stiff_ref, pot_ref, conn_ref, faces_ref, out_ref, *scratch):
+    hot, mine_ref, weight_ref, first_ref = scratch[0:4]
+    (got, sums, half, from_core, from_plane, line, total, gram, root, turned, back, acc, sent, came) = scratch[4:18]
     d = lax.axis_index("dom")
     s = lax.axis_index("st")
     core, y, z_lo = lax.rem(d, 2), lax.rem(lax.div(d, 2), 4), lax.div(d, 8)
@@ -322,10 +278,13 @@
         device(x=around(x, kx, 4), y=around(y, ky, 4)) for kx in range(4) for ky in range(4) if kx + ky]
     peers += [along_z(k) for k in range(1, 8)]
     peers += [device(x=around(x, k, 4), z_hi=1 - z_hi) for k in range(1, 4)]
+    peers += [{"dom": lax.rem(d + 1, doms)}, {"dom": lax.rem(d + doms - 1, doms)}]
     barrier = pltpu.get_barrier_semaphore()
     for peer in peers:
         pl.semaphore_signal(barrier, inc=1, device_id=peer, device_id_type=MESH_ID)
-    pl.semaphore_wait(barrier, len(peers))
+    filter_states(
+        doms, lambda: pl.semaphore_wait(barrier, len(peers)), bounds, scale, x_ref, stiff_ref, pot_ref, conn_ref,
+        faces_ref, mine_ref, weight_ref, first_ref, hot, *scratch[18:])
 
     def pair_rows(at):
         return pl.ds(pl.multiple_of(at * 128, 128), 128)
@@ -485,41 +444,62 @@
             out_ref[...] = (acc[...] + term).astype(bf16)
 
 
-def finished(states, weight, first):
+def body(doms, start_states, stiffness, cell_scale, potential, connectivity, shared_nodes, filter_bounds):
     vmem = pl.BlockSpec(memory_space=pltpu.VMEM)
+    smem = pl.BlockSpec(memory_space=pltpu.SMEM)
     copies = 11 + 1 + 15 + 7 + 15 + 3 + 3
+    finish_scratch = [
+        pltpu.VMEM((ENT, LNP), bf16),
+        pltpu.VMEM((512, NPC), bf16),
+        pltpu.VMEM((1, ENT), f32),
+        pltpu.VMEM((1, ENT), jnp.int32),
+        pltpu.VMEM((8, 128, NPC), bf16),
+        pltpu.VMEM((2, 256, 256), f32),
+        pltpu.VMEM((2, 256, 256), bf16),
+        pltpu.VMEM((256, 256), bf16),
+        pltpu.VMEM((15, 16, 256), bf16),
+        pltpu.VMEM((8, 16, 256), bf16),
+        pltpu.VMEM((3, 256, 256), bf16),
+        pltpu.VMEM((512, 512), f32),
+        pltpu.VMEM((512, 512), f32),
+        pltpu.VMEM((4, 128, NPC), bf16),
+        pltpu.VMEM((4, 128, NPC), bf16),
+        pltpu.VMEM((64, LNP), f32),
+        pltpu.SemaphoreType.DMA((copies,)),
+        pltpu.SemaphoreType.DMA((copies,)),
+    ]
+    filter_scratch = [
+        pltpu.VMEM((1, ENT), jnp.int32),
+        pltpu.VMEM((2, FACE), jnp.int32),
+        pltpu.VMEM((32, 128), f32),
+        pltpu.VMEM((128, 32), f32),
+        pltpu.VMEM((128, ENT), bf16),
+        pltpu.VMEM((32, ENT), bf16),
+        pltpu.VMEM((512, ENT), bf16),
+        pltpu.VMEM((1, ENT), jnp.int32),
+        pltpu.VMEM((1, ENT), jnp.int32),
+        pltpu.VMEM((1, ENT), f32),
+        pltpu.VMEM((128, ENT), bf16),
+        pltpu.VMEM((128, SPEC), bf16),
+        pltpu.VMEM((64, 2 * FACE), f32),
+        pltpu.VMEM((64, ENT), f32),
+        pltpu.VMEM((64, ENT), f32),
+        pltpu.VMEM((2, 512, NPC), bf16),
+        pltpu.VMEM((DEGREE, 2, 64, FACE), bf16),
+        pltpu.VMEM((DEGREE, 2, 64, FACE), bf16),
+        pltpu.SemaphoreType.DMA((DEGREE, 2)),
+        pltpu.SemaphoreType.DMA((DEGREE, 2)),
+    ]
     return pl.pallas_call(
-        finish_kernel,
+        functools.partial(kernel, doms),
         out_shape=jax.ShapeDtypeStruct((64, LNP), bf16),
-        in_specs=[vmem] * 3,
+        in_specs=[smem, smem] + [vmem] * 5,
         out_specs=vmem,
-        scratch_shapes=[
-            pltpu.VMEM((8, 128, NPC), bf16),
-            pltpu.VMEM((ENT, LNP), bf16),
-            pltpu.VMEM((2, 256, 256), f32),
-            pltpu.VMEM((2, 256, 256), bf16),
-            pltpu.VMEM((256, 256), bf16),
-            pltpu.VMEM((15, 16, 256), bf16),
-            pltpu.VMEM((8, 16, 256), bf16),
-            pltpu.VMEM((3, 256, 256), bf16),
-            pltpu.VMEM((512, 512), f32),
-            pltpu.VMEM((512, 512), f32),
-            pltpu.VMEM((4, 128, NPC), bf16),
-            pltpu.VMEM((4, 128, NPC), bf16),
-            pltpu.VMEM((64, LNP), f32),
-            pltpu.SemaphoreType.DMA((copies,)),
-            pltpu.SemaphoreType.DMA((copies,)),
-        ],
+        scratch_shapes=finish_scratch + filter_scratch,
         compiler_params=pltpu.CompilerParams(
-            collective_id=1, has_side_effects=True, vmem_limit_bytes=56 << 20),
-        name="finish",
-    )(states, weight, first)
-
-
-def body(doms, start_states, stiffness, cell_scale, potential, connectivity, shared_nodes, filter_bounds):
-    states, weight, first = filtered(
-        start_states, stiffness, cell_scale, potential, connectivity, shared_nodes, filter_bounds, doms)
-    return finished(states, weight, first)
+            collective_id=0, has_side_effects=True, vmem_limit_bytes=58 << 20),
+        name="subspace_step",
+    )(filter_bounds, cell_scale, start_states, stiffness, potential, connectivity, shared_nodes)
 
 
 def solution(mesh):

time: 107 us -> 98.4 us (0.920)
  Pallas kernels: 105 us -> 96.4 us
    pallas_call x2 -> x1, Pallas kernels: 105 us -> 96.4 us  [body(): pl.pallas_call(functools.partial(kernel, doms), out_shape=jax.ShapeDtypeS...]
where the time goes in v3:
time: 98.4 us; the launch traced here: 98.3 us
  Pallas kernels  96.4 us (98%)
  local copies, waits for them, and re-layouts  1.82 us (2%)
    pallas_call x1, Pallas kernels, body(): pl.pallas_call(functools.partial(kernel, doms), out_shape=jax.ShapeDtypeS...  96.4 us

profile of v3, /device:TPU:1, one launch (start us, length us, event | category | flops | bytes accessed | tf_op | source)
XLA Modules:
  0.0 98.3 jit_solution(17067595727175996973)
XLA Ops:
  0.0 96.4 %subspace_step.1 = bf16[64,3584]{1,0:T(8,128)(2,1)} custom-call(f32[2]{0:T(128)} %bounds.1, f32[8]{0:T(128)} %scale.1, bf16[64,3584]{1,0:T(8,128)(2,1)} %x_ref.1, bf16[512,512]{1,0:T(8,128)(2,1)} %stiff_ref.1, f32[3584]{0:T(1024)} %pot_ref.1, s32[8,512]{1,0:T(8,128)} %conn_ref.1, s32[1,2,435]{2,1,0:T(2,128)} %faces_ref.1), custom_call_target="tpu_custom_call" | custom-call | tf_op jit(solution)/shard_map/subspace_step/pallas_call | solution.py:493
  96.4 1.8 %copy.9 = bf16[64,3584]{1,0:T(8,128)(2,1)} copy(bf16[64,3584]{1,0:T(8,128)(2,1)} %subspace_step.1) | data formatting | bytes 917504

commit v4 on v3

--- a/solution.py
+++ b/solution.py
@@ -88,7 +88,7 @@
 
 
 def filter_states(
-    doms, wait_for_peers, bounds, scale, x_ref, stiff_ref, pot_ref, conn_ref, faces_ref,
+    doms, wait_for_peers, early_half, half_ready, bounds, scale, x_ref, stiff_ref, pot_ref, conn_ref, faces_ref,
     out_ref, weight_ref, first_ref,
     big, nodes, faces, pot_rows, pot_tab, oa, ob, hot, qa_ref, qb_ref, wpot_ref, parts, rows, sums, local, spread, field,
     send, recv, send_sem, recv_sem,
@@ -196,8 +196,14 @@
         high, low = split(both[0:64] + both[64:128])
         rows[0:64, 2 * FACE : SPEC] = high
         rows[64:128, 2 * FACE : SPEC] = low
+        last = step == DEGREE - 1
+        order = (early_half, 1 - early_half) if last else (0, 1)
+
+        def special_rows(h, begin, size):
+            return pl.ds(pl.multiple_of(h * SPEC + begin, FACE), size)
+
         others = [
-            dot(rows[:, 2 * FACE : SPEC], big[h * SPEC + 2 * FACE : (h + 1) * SPEC, SPEC:LNP]) for h in range(2)]
+            dot(rows[:, 2 * FACE : SPEC], big[special_rows(h, 2 * FACE, FACE), SPEC:LNP]) for h in order]
 
         @pl.when(has_left)
         def _():
@@ -215,20 +221,22 @@
             high, low = split(sums[:, part] + came)
             rows[0:64, part] = high
             rows[64:128, part] = low
-        for h in range(2):
-            both = others[h] + dot(rows[:, 0 : 2 * FACE], big[h * SPEC : h * SPEC + 2 * FACE, SPEC:LNP])
-            spread[:, h * HALF : (h + 1) * HALF] = both[0:64] + both[64:128]
-        for c in range(CELLS):
-            part = slice(c * NPC, (c + 1) * NPC)
-            block_rows = slice(c * 64, (c + 1) * 64)
-            h = jnp.where(qa_ref[:, part] >= 0, spread[:, part], local[:, part])
-            fresh = (h - center * now[block_rows].astype(f32)) / half_width
-            if step > 0:
-                fresh = 2.0 * fresh - old[block_rows].astype(f32)
-            if step == DEGREE - 1:
-                out_ref[block_rows] = fresh.astype(bf16)
-            else:
-                old[block_rows] = fresh.astype(bf16)
+        for h, other in zip(order, others):
+            both = other + dot(rows[:, 0 : 2 * FACE], big[special_rows(h, 0, 2 * FACE), SPEC:LNP])
+            spread[...] = both[0:64] + both[64:128]
+            for k in range(CELLS // 2):
+                part = pl.ds(pl.multiple_of((4 * h + k) * NPC, NPC), NPC)
+                block_rows = pl.ds(pl.multiple_of((4 * h + k) * 64, 64), 64)
+                hv = jnp.where(qa_ref[:, part] >= 0, spread[:, k * NPC : (k + 1) * NPC], local[:, part])
+                fresh = (hv - center * now[block_rows].astype(f32)) / half_width
+                if step > 0:
+                    fresh = 2.0 * fresh - old[block_rows].astype(f32)
+                if last:
+                    out_ref[block_rows] = fresh.astype(bf16)
+                else:
+                    old[block_rows] = fresh.astype(bf16)
+            if last and h is early_half:
+                half_ready()
 
 
 def product(a, b):
@@ -282,35 +290,26 @@
     barrier = pltpu.get_barrier_semaphore()
     for peer in peers:
         pl.semaphore_signal(barrier, inc=1, device_id=peer, device_id_type=MESH_ID)
+
+    def cell_rows(at, k):
+        return pl.ds(pl.multiple_of((at + 4 * k) * 64, 64), 64)
+
+    def place(k):
+        return pl.ds(pl.multiple_of(k * 64, 64), 64)
+
+    def to_block(by, k, z_there):
+        there = around(x, by, 4)
+        return copy(mine_ref.at[cell_rows(there, k)], got.at[s, place(k)], device(x=there, z_hi=z_there))
+
+    crossing = [to_block(by, 1 - z_hi, 1 - z_hi) for by in range(4)]
+    beside = [to_block(by, k, z_hi) for by in range(1, 4) for k in range(2)]
+    late = [to_block(by, z_hi, 1 - z_hi) for by in range(4)]
     filter_states(
-        doms, lambda: pl.semaphore_wait(barrier, len(peers)), bounds, scale, x_ref, stiff_ref, pot_ref, conn_ref,
-        faces_ref, mine_ref, weight_ref, first_ref, hot, *scratch[18:])
-
-    def pair_rows(at):
-        return pl.ds(pl.multiple_of(at * 128, 128), 128)
-
-    def cell_rows(at, k):
-        return pl.ds(pl.multiple_of(at * 128 + k * 64, 64), 64)
-
-    crossing = []
-    for k in range(4):
-        there = around(x, k, 4)
-        crossing.append(copy(
-            mine_ref.at[cell_rows(there, 1 - z_hi)], got.at[s, cell_rows(0, 1 - z_hi)],
-            device(x=there, z_hi=1 - z_hi)))
-    start(crossing)
-    beside = []
-    for k in range(1, 4):
-        there = around(x, k, 4)
-        beside.append(copy(mine_ref.at[pair_rows(there)], got.at[s], device(x=there)))
+        doms, lambda: pl.semaphore_wait(barrier, len(peers)), 1 - z_hi, lambda: start(crossing), bounds, scale, x_ref,
+        stiff_ref, pot_ref, conn_ref, faces_ref, mine_ref, weight_ref, first_ref, hot, *scratch[18:])
     start(beside)
-    late = []
-    for k in range(4):
-        there = around(x, k, 4)
-        late.append(copy(
-            mine_ref.at[cell_rows(there, z_hi)], got.at[s, cell_rows(0, z_hi)],
-            device(x=there, z_hi=1 - z_hi)))
-    got[s] = mine_ref[pair_rows(x)]
+    for k in range(2):
+        got[s, place(k)] = mine_ref[cell_rows(x, k)]
 
     lane = lax.broadcasted_iota(jnp.int32, (128, 128), 1)
 
@@ -324,8 +323,6 @@
             mine = jnp.where(block == j, 1.0, 0.0).astype(bf16)
             hot[at, j * 128 : (j + 1) * 128] = low * mine
 
-    finish(crossing)
-    start(late[0:2])
     finish(beside)
 
     def weighted(rows, at):
@@ -335,14 +332,16 @@
     own = pl.ds(pl.multiple_of(z_hi * 4, 4), 4)
     first_cell = got[own, 0:64].reshape(256, NPC)
     second_cell = got[own, 64:128].reshape(256, NPC)
-    sums[0] = contract_last(weighted(first_cell, 2 * x), first_cell) + contract_last(
-        weighted(second_cell, 2 * x + 1), second_cell)
+    sums[0] = contract_last(weighted(first_cell, x), first_cell) + contract_last(
+        weighted(second_cell, x + 4), second_cell)
+    half[0] = sums[0].astype(bf16)
+    finish(crossing)
+    start(late[0:2])
     shared_rows = pl.ds(pl.multiple_of(z_hi * 64, 64), 64)
     low_half = got[0:4, shared_rows].reshape(256, NPC)
     high_half = got[4:8, shared_rows].reshape(256, NPC)
-    sums[1] = contract_last(weighted(low_half, 2 * x + z_hi), high_half)
-
-    half[0] = sums[0].astype(bf16)
+    sums[1] = contract_last(weighted(low_half, x + 4 * z_hi), high_half)
+
     half[1] = sums[1].astype(bf16)
     finish(start([copy(half.at[1 - core], from_core, device(core=1 - core))]))
     sums[core] = sums[core] + from_core[...].astype(f32)
@@ -380,29 +379,30 @@
     count[0] -= len(plane)
     held_one = [copy(total.at[2, piece_rows], total.at[2, piece_rows], in_plane(*by)) for by in plane]
 
+    came_from = [piece_rows] + [piece_of(4 - kx, 4 - ky) for kx, ky in plane]
+    other_core = device(core=1 - core)
+    passed = [copy(total.at[pl.ds(0, 2), at], total.at[pl.ds(0, 2), at], other_core) for at in came_from]
+    count[0] -= len(came_from)
+    passed_one = [copy(total.at[2, at], total.at[2, at], other_core) for at in came_from]
+
+    def pass_on(arriving, onward, awaited):
+        start(arriving)
+        onward[0].start()
+        for one, after in zip(arriving, onward[1:]):
+            one.wait_recv()
+            after.start()
+        for one in arriving + onward:
+            one.wait_send()
+        for one in awaited:
+            one.wait_recv()
+
     @pl.when(core == 0)
     def _():
-        finish(start(held))
+        pass_on(held, passed, passed_one)
 
     @pl.when(core == 1)
     def _():
-        finish(start(held_one))
-
-    down = [copy(total.at[k], total.at[k], device(core=1 - core)) for k in range(3)]
-
-    @pl.when(core == 0)
-    def _():
-        start(down[0:2])
-        for one in down[0:2]:
-            one.wait_send()
-        down[2].wait_recv()
-
-    @pl.when(core == 1)
-    def _():
-        start(down[2:3])
-        down[2].wait_send()
-        for one in down[0:2]:
-            one.wait_recv()
+        pass_on(held_one, passed_one, passed)
 
     upper = total[2].astype(f32)
     gram[0:256, 0:256] = total[0].astype(f32)
@@ -434,8 +434,8 @@
         source = around(x, 4 - k, 4)
         if k:
             returned[k - 1].wait()
-        pair = jnp.concatenate([back[source, 0:64], back[source, 64:128]], axis=1)
-        term = dot(pair, hot[pl.ds(pl.multiple_of(source * 1024, 1024), 1024)])
+        term = dot(back[source, 0:64], hot[pl.ds(pl.multiple_of(source * NPC, NPC), NPC)]) + dot(
+            back[source, 64:128], hot[pl.ds(pl.multiple_of((source + 4) * NPC, NPC), NPC)])
         if k == 0:
             acc[...] = term
         elif k < 3:
@@ -447,7 +447,7 @@
 def body(doms, start_states, stiffness, cell_scale, potential, connectivity, shared_nodes, filter_bounds):
     vmem = pl.BlockSpec(memory_space=pltpu.VMEM)
     smem = pl.BlockSpec(memory_space=pltpu.SMEM)
-    copies = 11 + 1 + 15 + 7 + 15 + 3 + 3
+    copies = 14 + 1 + 15 + 7 + 15 + 16 + 3
     finish_scratch = [
         pltpu.VMEM((ENT, LNP), bf16),
         pltpu.VMEM((512, NPC), bf16),
@@ -483,7 +483,7 @@
         pltpu.VMEM((128, SPEC), bf16),
         pltpu.VMEM((64, 2 * FACE), f32),
         pltpu.VMEM((64, ENT), f32),
-        pltpu.VMEM((64, ENT), f32),
+        pltpu.VMEM((64, HALF), f32),
         pltpu.VMEM((2, 512, NPC), bf16),
         pltpu.VMEM((DEGREE, 2, 64, FACE), bf16),
         pltpu.VMEM((DEGREE, 2, 64, FACE), bf16),

time: 98.4 us -> 103 us (1.047)
  Pallas kernels: 96.4 us -> 101 us
    pallas_call x1, Pallas kernels: 96.4 us -> 101 us  [body(): pl.pallas_call(functools.partial(kernel, doms), out_shape=jax.ShapeDtypeS...]
where the time goes in v4:
time: 103 us; the launch traced here: 102 us
  Pallas kernels  101 us (98%)
  local copies, waits for them, and re-layouts  1.82 us (2%)
    pallas_call x1, Pallas kernels, body(): pl.pallas_call(functools.partial(kernel, doms), out_shape=jax.ShapeDtypeS...  101 us

profile of v4, /device:TPU:1, one launch (start us, length us, event | category | flops | bytes accessed | tf_op | source)
XLA Modules:
  0.0 102.5 jit_solution(1123909662041163373)
XLA Ops:
  0.0 100.6 %subspace_step.1 = bf16[64,3584]{1,0:T(8,128)(2,1)} custom-call(f32[2]{0:T(128)} %bounds.1, f32[8]{0:T(128)} %scale.1, bf16[64,3584]{1,0:T(8,128)(2,1)} %x_ref.1, bf16[512,512]{1,0:T(8,128)(2,1)} %stiff_ref.1, f32[3584]{0:T(1024)} %pot_ref.1, s32[8,512]{1,0:T(8,128)} %conn_ref.1, s32[1,2,435]{2,1,0:T(2,128)} %faces_ref.1), custom_call_target="tpu_custom_call" | custom-call | tf_op jit(solution)/shard_map/subspace_step/pallas_call | solution.py:493
  100.7 1.8 %copy.9 = bf16[64,3584]{1,0:T(8,128)(2,1)} copy(bf16[64,3584]{1,0:T(8,128)(2,1)} %subspace_step.1) | data formatting | bytes 917504

commit v5 on v3

--- a/solution.py
+++ b/solution.py
@@ -324,8 +324,6 @@
             mine = jnp.where(block == j, 1.0, 0.0).astype(bf16)
             hot[at, j * 128 : (j + 1) * 128] = low * mine
 
-    finish(crossing)
-    start(late[0:2])
     finish(beside)
 
     def weighted(rows, at):
@@ -337,12 +335,14 @@
     second_cell = got[own, 64:128].reshape(256, NPC)
     sums[0] = contract_last(weighted(first_cell, 2 * x), first_cell) + contract_last(
         weighted(second_cell, 2 * x + 1), second_cell)
+    half[0] = sums[0].astype(bf16)
+    finish(crossing)
+    start(late[0:2])
     shared_rows = pl.ds(pl.multiple_of(z_hi * 64, 64), 64)
     low_half = got[0:4, shared_rows].reshape(256, NPC)
     high_half = got[4:8, shared_rows].reshape(256, NPC)
     sums[1] = contract_last(weighted(low_half, 2 * x + z_hi), high_half)
 
-    half[0] = sums[0].astype(bf16)
     half[1] = sums[1].astype(bf16)
     finish(start([copy(half.at[1 - core], from_core, device(core=1 - core))]))
     sums[core] = sums[core] + from_core[...].astype(f32)
@@ -380,29 +380,30 @@
     count[0] -= len(plane)
     held_one = [copy(total.at[2, piece_rows], total.at[2, piece_rows], in_plane(*by)) for by in plane]
 
+    came_from = [piece_rows] + [piece_of(4 - kx, 4 - ky) for kx, ky in plane]
+    other_core = device(core=1 - core)
+    passed = [copy(total.at[pl.ds(0, 2), at], total.at[pl.ds(0, 2), at], other_core) for at in came_from]
+    count[0] -= len(came_from)
+    passed_one = [copy(total.at[2, at], total.at[2, at], other_core) for at in came_from]
+
+    def pass_on(arriving, onward, awaited):
+        start(arriving)
+        onward[0].start()
+        for one, after in zip(arriving, onward[1:]):
+            one.wait_recv()
+            after.start()
+        for one in arriving + onward:
+            one.wait_send()
+        for one in awaited:
+            one.wait_recv()
+
     @pl.when(core == 0)
     def _():
-        finish(start(held))
+        pass_on(held, passed, passed_one)
 
     @pl.when(core == 1)
     def _():
-        finish(start(held_one))
-
-    down = [copy(total.at[k], total.at[k], device(core=1 - core)) for k in range(3)]
-
-    @pl.when(core == 0)
-    def _():
-        start(down[0:2])
-        for one in down[0:2]:
-            one.wait_send()
-        down[2].wait_recv()
-
-    @pl.when(core == 1)
-    def _():
-        start(down[2:3])
-        down[2].wait_send()
-        for one in down[0:2]:
-            one.wait_recv()
+        pass_on(held_one, passed_one, passed)
 
     upper = total[2].astype(f32)
     gram[0:256, 0:256] = total[0].astype(f32)
@@ -447,7 +448,7 @@
 def body(doms, start_states, stiffness, cell_scale, potential, connectivity, shared_nodes, filter_bounds):
     vmem = pl.BlockSpec(memory_space=pltpu.VMEM)
     smem = pl.BlockSpec(memory_space=pltpu.SMEM)
-    copies = 11 + 1 + 15 + 7 + 15 + 3 + 3
+    copies = 11 + 1 + 15 + 7 + 15 + 16 + 3
     finish_scratch = [
         pltpu.VMEM((ENT, LNP), bf16),
         pltpu.VMEM((512, NPC), bf16),

time: 98.4 us -> 97.8 us (level)
  no operation moved by 1% of the time
where the time goes in v5:
time: 97.8 us; the launch traced here: 97.7 us
  Pallas kernels  95.9 us (98%)
  local copies, waits for them, and re-layouts  1.82 us (2%)
    pallas_call x1, Pallas kernels, body(): pl.pallas_call(functools.partial(kernel, doms), out_shape=jax.ShapeDtypeS...  95.9 us

profile of v5, /device:TPU:1, one launch (start us, length us, event | category | flops | bytes accessed | tf_op | source)
XLA Modules:
  0.0 97.7 jit_solution(16947250109507975658)
XLA Ops:
  0.0 95.9 %subspace_step.1 = bf16[64,3584]{1,0:T(8,128)(2,1)} custom-call(f32[2]{0:T(128)} %bounds.1, f32[8]{0:T(128)} %scale.1, bf16[64,3584]{1,0:T(8,128)(2,1)} %x_ref.1, bf16[512,512]{1,0:T(8,128)(2,1)} %stiff_ref.1, f32[3584]{0:T(1024)} %pot_ref.1, s32[8,512]{1,0:T(8,128)} %conn_ref.1, s32[1,2,435]{2,1,0:T(2,128)} %faces_ref.1), custom_call_target="tpu_custom_call" | custom-call | tf_op jit(solution)/shard_map/subspace_step/pallas_call | solution.py:494
  95.9 1.8 %copy.9 = bf16[64,3584]{1,0:T(8,128)(2,1)} copy(bf16[64,3584]{1,0:T(8,128)(2,1)} %subspace_step.1) | data formatting | bytes 917504
